TPU v7x, 256 devices: a whole 4x4x8 slice. The times are simulated.
256 devices in a mesh: seg: 4 (over x), sec: 32 (over z, y), rep: 2 (over core).
Axes of the slice: x: 4, y: 4, z: 8, core: 2. Of those that a mesh axis runs over, the one named last changes fastest.
Arguments:
- psi: float32 [4, 64, 256, 256], P('seg', 'sec'), may hold values from -6 to 6
- left_env: bfloat16 [4, 18, 64, 256, 256], P('seg', 'rep', 'sec'), may hold values from -0.375 to 0.375
- right_env: bfloat16 [4, 18, 64, 256, 256], P('seg', 'rep', 'sec'), may hold values from -0.375 to 0.375
- local_block: bfloat16 [4, 64, 256, 256], P('seg', 'sec'), may hold values from -0.375 to 0.375
- kept_left: int32 [4, 64], P('seg', 'sec'), may hold values from 64 to 256
- kept_right: int32 [4, 64], P('seg', 'sec'), may hold values from 64 to 256
- pattern: int32 [4, 18, 64], P('seg', 'rep', 'sec'), may hold values 0 or 1
- term_charge: int32 [18], replicated, may hold values from -2 to 2
Outputs:
- last_vector: float32 [4, 64, 256, 256], P('seg', 'sec')
- coefficients: float32 [4, 8], P('seg')
All inputs are finite; a program needn't handle non-finite values. No bound on the sum of `pattern` on one device may be relied on, other than what follows from the above.
Results may differ from a plain program's by a relative error of at most 0.012.
Values may be sent and summed in bfloat16 or wider, within the bound.
A program may use at most 64 MiB of HBM per device.

v0:
```python
import jax
import jax.numpy as jnp
from jax import lax
from jax.sharding import PartitionSpec as P

ITERS = 4


def extended_2(shard, sides, width):
    for axis, dim in sides:
        size, length = (lax.axis_size(axis), shard.shape[dim])
        up = [(i, (i + 1) % size) for i in range(size - 1)]
        down = [(j, i) for i, j in up]
        last = lax.slice_in_dim(shard, length - width, length, axis=dim)
        first = lax.slice_in_dim(shard, 0, width, axis=dim)
        before = lax.ppermute(last, axis, up)
        after = lax.ppermute(first, axis, down)
        shard = jnp.concatenate([before, shard, after], axis=dim)
    return shard


def from_behind(shard, axis, by):
    length = lax.axis_size(axis)
    return lax.ppermute(shard, axis, [(i, (i + by) % length) for i in range(length)])


def widen(vb):
    return extended_2(vb, (("sec", 0),), 2)


def shifted(extended, charges, first, number):
    index = first + 2 + lax.iota(jnp.int32, number)[None, :] + charges[:, None]
    return extended[index]


def term_action(moved, lefts, rights, pat):
    inner = jnp.einsum("wsij,wsjk->wsik", lefts, moved, preferred_element_type=jnp.float32)
    inner = (inner * pat[:, :, None, None]).astype(jnp.bfloat16)
    return jnp.einsum("wsik,wslk->sil", inner, rights, preferred_element_type=jnp.float32)


def local_action(vb, block):
    first = jnp.einsum("sij,sjk->sik", block, vb, preferred_element_type=jnp.float32)
    return first + jnp.einsum("sij,skj->sik", vb, block, preferred_element_type=jnp.float32)


def lanczos(start, apply_op, mean_of):
    vector = start / jnp.sqrt(mean_of(start * start) + 1e-06)
    prev = jnp.zeros_like(vector)
    beta_prev = jnp.float32(0.0)
    alphas = []
    betas = []
    for step in range(ITERS):
        image = apply_op(vector)
        alpha = mean_of(vector * image)
        image = image - alpha * vector - beta_prev * prev
        beta = jnp.sqrt(mean_of(image * image) + 1e-06)
        prev = vector
        vector = image / beta
        beta_prev = beta
        alphas.append(alpha)
        betas.append(beta)
    return (vector, jnp.stack(alphas + betas))


def on_device(psi, left_env, right_env, local_block, kept_left, kept_right, pattern, term_charge):
    lefts = from_behind(left_env, "seg", 1)[0]
    rights = from_behind(right_env, "seg", -1)[0]
    start = psi[0]
    block = local_block[0]
    width = start.shape[1]
    sectors = start.shape[0]
    terms_here = lefts.shape[0]
    states = lax.iota(jnp.int32, width)
    rows = (states[None, :] < kept_left[0][:, None]).astype(jnp.float32)
    cols = (states[None, :] < kept_right[0][:, None]).astype(jnp.float32)
    projector = rows[:, :, None] * cols[:, None, :]
    count = sectors * lax.axis_size("sec") * width * width
    local_charge = lax.dynamic_slice_in_dim(
        term_charge, lax.axis_index("rep") * terms_here, terms_here, 0
    )
    pat = pattern[0].astype(jnp.float32)

    def apply_whole(vector):
        vb = vector.astype(jnp.bfloat16)
        moved = shifted(widen(vb), local_charge, 0, sectors)
        total = lax.psum(term_action(moved, lefts, rights, pat).astype(jnp.bfloat16), "rep").astype(
            jnp.float32
        )
        return projector * (total + local_action(vb, block))

    def mean_whole(values):
        return lax.psum(jnp.sum(values), "sec") / count

    vector, coeffs = lanczos(projector * start, apply_whole, mean_whole)
    return (vector[None], coeffs[None])


def solution(mesh):
    placed = (
        P("seg", "sec", None, None),
        P("seg", "rep", "sec", None, None),
        P("seg", "rep", "sec", None, None),
        P("seg", "sec", None, None),
        P("seg", "sec"),
        P("seg", "sec"),
        P("seg", "rep", "sec"),
        P(),
    )
    return jax.shard_map(
        on_device,
        mesh=mesh,
        in_specs=placed,
        out_specs=(P("seg", "sec", None, None), P("seg", None)),
        check_vma=False,
    )
```

profile of v0, /device:TPU:8, one launch (start us, length us, event | category | flops | bytes accessed | tf_op | source)
XLA Modules:
  0.0 898.0 jit_solution(11741691733564219125)
XLA Ops:
  7.3 3.4 copy.19
  10.7 2.8 collective-permute-start.3
  14.3 74.4 %psum.91 = f32[]{:T(128)} all-reduce(f32[]{:T(128)} %multiply_reduce_fusion.8), channel_id=1, replica_groups=mesh['seg'=4,'sec'=32,'rep'=2] {'sec'}, use_global_device_ids=true, to_apply=%region_1.0 | all-reduce | flops 1 | bytes 8 | tf_op jit(solution)/shard_map/psum | solution.py:93
  89.6 3.2 collective-permute-start
  92.8 4.6 collective-permute-start.1
  103.7 5.2 fusion.104
  109.2 32.2 %all-reduce.5.cloned.1.call-done = bf16[2,256,256]{2,1,0:T(8,128)(2,1)} async-done(((bf16[2,256,256]{2,1,0:T(8,128)(2,1)}), bf16[2,256,256]{2,1,0:T(8,128)(2,1)}) %all-reduce.5.cloned.1.call-update) | async-done | bytes 262160 | tf_op jit(solution)/shard_map/psum | solution.py:87
  143.4 71.8 %psum.93 = f32[]{:T(128)} all-reduce(f32[]{:T(128)} %get-tuple-element.10), channel_id=1, replica_groups=mesh['seg'=4,'sec'=32,'rep'=2] {'sec'}, use_global_device_ids=true, to_apply=%region_4.0 | all-reduce | flops 1 | bytes 8 | tf_op jit(solution)/shard_map/psum | solution.py:93
  216.7 74.8 %psum.94 = f32[]{:T(128)} all-reduce(f32[]{:T(128)} %multiply_reduce_fusion.6), channel_id=1, replica_groups=mesh['seg'=4,'sec'=32,'rep'=2] {'sec'}, use_global_device_ids=true, to_apply=%region_6.0 | all-reduce | flops 1 | bytes 8 | tf_op jit(solution)/shard_map/psum | solution.py:93
  294.3 3.9 collective-permute-start.5
  305.0 5.2 fusion.113
  310.5 30.3 %all-reduce.7.cloned.1.call-done = bf16[2,256,256]{2,1,0:T(8,128)(2,1)} async-done(((bf16[2,256,256]{2,1,0:T(8,128)(2,1)}), bf16[2,256,256]{2,1,0:T(8,128)(2,1)}) %all-reduce.7.cloned.1.call-update) | async-done | bytes 262160 | tf_op jit(solution)/shard_map/psum | solution.py:87
  342.8 71.8 %psum.96 = f32[]{:T(128)} all-reduce(f32[]{:T(128)} %get-tuple-element.12), channel_id=1, replica_groups=mesh['seg'=4,'sec'=32,'rep'=2] {'sec'}, use_global_device_ids=true, to_apply=%region_9.0 | all-reduce | flops 1 | bytes 8 | tf_op jit(solution)/shard_map/psum | solution.py:93
  416.1 74.8 %psum.97 = f32[]{:T(128)} all-reduce(f32[]{:T(128)} %get-tuple-element.6), channel_id=1, replica_groups=mesh['seg'=4,'sec'=32,'rep'=2] {'sec'}, use_global_device_ids=true, to_apply=%region_11.0 | all-reduce | flops 1 | bytes 8 | tf_op jit(solution)/shard_map/psum | solution.py:93
  493.6 3.9 collective-permute-start.7
  504.3 5.2 fusion.122
  509.8 30.3 %all-reduce.9.cloned.1.call-done = bf16[2,256,256]{2,1,0:T(8,128)(2,1)} async-done(((bf16[2,256,256]{2,1,0:T(8,128)(2,1)}), bf16[2,256,256]{2,1,0:T(8,128)(2,1)}) %all-reduce.9.cloned.1.call-update) | async-done | bytes 262160 | tf_op jit(solution)/shard_map/psum | solution.py:87
  542.1 71.8 %psum.99 = f32[]{:T(128)} all-reduce(f32[]{:T(128)} %get-tuple-element.14), channel_id=1, replica_groups=mesh['seg'=4,'sec'=32,'rep'=2] {'sec'}, use_global_device_ids=true, to_apply=%region_14.0 | all-reduce | flops 1 | bytes 8 | tf_op jit(solution)/shard_map/psum | solution.py:93
  615.3 74.8 %psum.100 = f32[]{:T(128)} all-reduce(f32[]{:T(128)} %get-tuple-element.4), channel_id=1, replica_groups=mesh['seg'=4,'sec'=32,'rep'=2] {'sec'}, use_global_device_ids=true, to_apply=%region_16.0 | all-reduce | flops 1 | bytes 8 | tf_op jit(solution)/shard_map/psum | solution.py:93
  692.8 4.1 collective-permute-start.9
  703.5 5.2 fusion.131
  709.0 30.4 %all-reduce.11.cloned.1.call-done = bf16[2,256,256]{2,1,0:T(8,128)(2,1)} async-done(((bf16[2,256,256]{2,1,0:T(8,128)(2,1)}), bf16[2,256,256]{2,1,0:T(8,128)(2,1)}) %all-reduce.11.cloned.1.call-update) | async-done | bytes 262160 | tf_op jit(solution)/shard_map/psum | solution.py:87
  741.3 71.8 %psum.102 = f32[]{:T(128)} all-reduce(f32[]{:T(128)} %get-tuple-element.16), channel_id=1, replica_groups=mesh['seg'=4,'sec'=32,'rep'=2] {'sec'}, use_global_device_ids=true, to_apply=%region_19.0 | all-reduce | flops 1 | bytes 8 | tf_op jit(solution)/shard_map/psum | solution.py:93
  814.6 74.8 %psum.103 = f32[]{:T(128)} all-reduce(f32[]{:T(128)} %get-tuple-element.2), channel_id=1, replica_groups=mesh['seg'=4,'sec'=32,'rep'=2] {'sec'}, use_global_device_ids=true, to_apply=%region_21.0 | all-reduce | flops 1 | bytes 8 | tf_op jit(solution)/shard_map/psum | solution.py:93
  (76 shorter events, 47.4 us)
Async XLA Ops:
  7.2 101.8 %copy-start = (bf16[1,2,256,256]{3,2,1,0:T(8,128)(2,1)S(1)}, bf16[1,2,256,256]{3,2,1,0:T(8,128)(2,1)}, u32[]{:S(2)}) copy-start(bf16[1,2,256,256]{3,2,1,0:T(8,128)(2,1)} %param.11) | copy-start | bytes 786436
  7.2 6.3 copy-start.8
  7.2 6.2 copy-start.7
  7.2 6.3 copy-start.1
  7.2 90.2 %copy-start.9 = (s32[18]{0:T(128)S(1)}, s32[18]{0:T(128)}, u32[]{:S(2)}) copy-start(s32[18]{0:T(128)} %param.15) | copy-start | bytes 220
  7.2 90.4 %copy-start.6 = (s32[1,9,2]{1,2,0:T(2,128)S(1)}, s32[1,9,2]{1,2,0:T(2,128)}, u32[]{:S(2)}) copy-start(s32[1,9,2]{1,2,0:T(2,128)} %param.14) | copy-start | bytes 220
  7.2 134.2 %all-reduce.5.cloned.1.call-start = ((), (), s32[]{:S(2)}) async-start(), calls=%async_computation | async-start | bytes 524288 | tf_op jit(solution)/shard_map/psum | solution.py:87
  10.7 93.0 %collective-permute-start.3 = (bf16[1,9,2,256,256]{4,3,1,2,0:T(8,128)(2,1)}, bf16[1,9,2,256,256]{4,3,1,2,0:T(8,128)(2,1)}, u32[]{:S(2)}, u32[]{:S(2)}) collective-permute-start(bf16[1,9,2,256,256]{4,3,1,2,0:T(8,128)(2,1)} %copy.19), channel_id=1, source_target_pairs={{0,192},{64,0},{128,64},{192,128},{1,193},{65,1},{129,65},{193,129... | collective-permute-start | bytes 7077896 | tf_op jit(solution)/shard_map/ppermute | solution.py:24
  13.4 90.3 %collective-permute-start.2 = (bf16[1,9,2,256,256]{4,3,2,1,0:T(8,128)(2,1)}, bf16[1,9,2,256,256]{4,3,2,1,0:T(8,128)(2,1)}, u32[]{:S(2)}, u32[]{:S(2)}) collective-permute-start(bf16[1,9,2,256,256]{4,3,2,1,0:T(8,128)(2,1)} %param.9), channel_id=1, source_target_pairs={{0,64},{64,128},{128,192},{192,0},{1,65},{65,129},{129,193},{193,1... | collective-permute-start | bytes 7077896 | tf_op jit(solution)/shard_map/ppermute | solution.py:24
  89.6 10.2 %collective-permute-start = (bf16[2,256,256]{2,1,0:T(8,128)(2,1)S(1)}, bf16[2,256,256]{2,1,0:T(8,128)(2,1)S(1)}, u32[]{:S(2)}, u32[]{:S(2)}) collective-permute-start(bf16[2,256,256]{2,1,0:T(8,128)(2,1)S(1)} %fusion.155), channel_id=1, source_target_pairs={{0,2},{2,4},{4,6},{6,8},{8,10},{10,12},{12,14},{14,16},{16,18},{18... | collective-permute-start | bytes 786440 | tf_op jit(solution)/shard_map/ppermute | solution.py:16
  92.8 8.5 collective-permute-start.1
  108.9 231.9 %all-reduce.7.cloned.1.call-start = ((), (), s32[]{:S(2)}) async-start(), calls=%async_computation.1 | async-start | bytes 524288 | tf_op jit(solution)/shard_map/psum | solution.py:87
  141.4 74.3 %copy-start.2 = (bf16[2,256,256]{2,1,0:T(8,128)(2,1)S(1)}, bf16[2,256,256]{2,1,0:T(8,128)(2,1)}, u32[]{:S(2)}) copy-start(bf16[2,256,256]{2,1,0:T(8,128)(2,1)} %all-reduce.5.cloned.1.call-done) | copy-start | bytes 786436
  292.4 8.3 collective-permute-start.4
  294.3 8.3 collective-permute-start.5
  310.2 229.9 %all-reduce.9.cloned.1.call-start = ((), (), s32[]{:S(2)}) async-start(), calls=%async_computation.2 | async-start | bytes 524288 | tf_op jit(solution)/shard_map/psum | solution.py:87
  340.9 74.3 %copy-start.3 = (bf16[2,256,256]{2,1,0:T(8,128)(2,1)S(1)}, bf16[2,256,256]{2,1,0:T(8,128)(2,1)}, u32[]{:S(2)}) copy-start(bf16[2,256,256]{2,1,0:T(8,128)(2,1)} %all-reduce.7.cloned.1.call-done) | copy-start | bytes 786436
  491.7 8.3 collective-permute-start.6
  493.6 8.3 collective-permute-start.7
  509.5 229.9 %all-reduce.11.cloned.1.call-start = ((), (), s32[]{:S(2)}) async-start(), calls=%async_computation.3 | async-start | bytes 524288 | tf_op jit(solution)/shard_map/psum | solution.py:87
  540.1 74.3 %copy-start.4 = (bf16[2,256,256]{2,1,0:T(8,128)(2,1)S(1)}, bf16[2,256,256]{2,1,0:T(8,128)(2,1)}, u32[]{:S(2)}) copy-start(bf16[2,256,256]{2,1,0:T(8,128)(2,1)} %all-reduce.9.cloned.1.call-done) | copy-start | bytes 786436
  690.9 8.3 collective-permute-start.8
  692.8 8.3 collective-permute-start.9
  739.4 74.3 %copy-start.5 = (bf16[2,256,256]{2,1,0:T(8,128)(2,1)S(1)}, bf16[2,256,256]{2,1,0:T(8,128)(2,1)}, u32[]{:S(2)}) copy-start(bf16[2,256,256]{2,1,0:T(8,128)(2,1)} %all-reduce.11.cloned.1.call-done) | copy-start | bytes 786436
Sparse Core Ops, SparseCore 0:
  109.0 32.3 all-reduce.4
  310.3 30.4 all-reduce.6
  509.6 30.4 all-reduce.8
  708.8 30.4 all-reduce.10
where the time goes:
time: 899 us; the launch traced here: 898 us
  blocking collectives  661 us (74%)
  waiting for transfers between devices  140 us (16%)
  matrix products  29.6 us (3%)
  starting transfers between devices  28.5 us (3%)
  between operations  20.1 us (2%)
  local copies, waits for them, and re-layouts  13.5 us (2%)
    psum x9, blocking collectives, mean_whole(): return lax.psum(jnp.sum(values), 'sec') / count  661 us
    psum x4, waiting for transfers between devices, apply_whole(): lax.psum(term_action(moved, lefts, rights, pat).astype(jnp.bfloat16), 'rep')  123 us
    dot_general x4, matrix products, term_action(): jnp.einsum('wsik,wslk->sil', inner, rights, preferred_element_type=jnp.fl...  20.8 us
  transfers between devices with their start and end apart: 14, of which 12 were waited for; matrix products, arithmetic and copies ran while one was open for 1% of the time, Pallas kernels for 0%

commit v1 on v0

--- a/solution.py
+++ b/solution.py
@@ -1,9 +1,18 @@
+import functools
 import jax
 import jax.numpy as jnp
 from jax import lax
 from jax.sharding import PartitionSpec as P
 
 ITERS = 4
+
+
+def extend_chunk_now(inner_x, along_axis):
+    z = lax.all_gather(inner_x, along_axis).sum(axis=0)
+    return z
+
+
+draw_regions_over_axis = functools.partial(extend_chunk_now, along_axis="rep")
 
 
 def extended_2(shard, sides, width):
@@ -84,9 +93,9 @@
     def apply_whole(vector):
         vb = vector.astype(jnp.bfloat16)
         moved = shifted(widen(vb), local_charge, 0, sectors)
-        total = lax.psum(term_action(moved, lefts, rights, pat).astype(jnp.bfloat16), "rep").astype(
-            jnp.float32
-        )
+        total = draw_regions_over_axis(
+            term_action(moved, lefts, rights, pat).astype(jnp.bfloat16)
+        ).astype(jnp.float32)
         return projector * (total + local_action(vb, block))
 
     def mean_whole(values):

time: 899 us -> 761 us (0.85)
  waiting for transfers between devices: 140 us -> 18.1 us
  between operations: 20.1 us -> 7.04 us
    psum x4 -> x0, waiting for transfers between devices: 123 us -> none  [apply_whole(): lax.psum(term_action(moved, lefts, rights, pat).astype(jnp.bfloat16), 'rep')]
    psum x9, blocking collectives: 661 us -> 645 us  [mean_whole(): return lax.psum(jnp.sum(values), 'sec') / count]
  transfers between devices with their start and end apart: 14 -> 10, of which waited for: 12 -> 8; matrix products, arithmetic and copies ran while one was open for 1% -> 1% of each run, Pallas kernels for 0% -> 0%
where the time goes in v1:
time: 761 us; the launch traced here: 753 us
  blocking collectives  653 us (86%)
  starting transfers between devices  28.6 us (4%)
  matrix products  22.9 us (3%)
  waiting for transfers between devices  18.1 us (2%)
  local copies, waits for them, and re-layouts  16.8 us (2%)
    psum x9, blocking collectives, mean_whole(): return lax.psum(jnp.sum(values), 'sec') / count  645 us
    dot_general x4, matrix products, term_action(): jnp.einsum('wsik,wslk->sil', inner, rights, preferred_element_type=jnp.fl...  18.2 us
  transfers between devices with their start and end apart: 10, of which 8 were waited for; matrix products, arithmetic and copies ran while one was open for 1% of the time, Pallas kernels for 0%

profile of v1, /device:TPU:8, one launch (start us, length us, event | category | flops | bytes accessed | tf_op | source)
XLA Modules:
  0.0 752.6 jit_solution(14964991319230918834)
XLA Ops:
  0.7 3.5 copy.35
  4.1 2.8 collective-permute-start.3
  9.6 74.5 %psum.63 = f32[]{:T(128)} all-reduce(f32[]{:T(128)} %multiply_reduce_fusion.8), channel_id=1, replica_groups=mesh['seg'=4,'sec'=32,'rep'=2] {'sec'}, use_global_device_ids=true, to_apply=%region_1.0 | all-reduce | flops 1 | bytes 8 | tf_op jit(solution)/shard_map/psum | solution.py:102
  85.0 6.4 collective-permute-start.1
  95.3 4.4 collective-permute-done
  99.7 2.3 gather_fusion
  102.0 4.6 fusion.108
  110.0 69.8 %psum.64 = f32[]{:T(128)} all-reduce(f32[]{:T(128)} %get-tuple-element.16), channel_id=1, replica_groups=mesh['seg'=4,'sec'=32,'rep'=2] {'sec'}, use_global_device_ids=true, to_apply=%region_4.0 | all-reduce | flops 1 | bytes 8 | tf_op jit(solution)/shard_map/psum | solution.py:102
  181.3 72.7 %psum.65 = f32[]{:T(128)} all-reduce(f32[]{:T(128)} %multiply_reduce_fusion.6), channel_id=1, replica_groups=mesh['seg'=4,'sec'=32,'rep'=2] {'sec'}, use_global_device_ids=true, to_apply=%region_6.0 | all-reduce | flops 1 | bytes 8 | tf_op jit(solution)/shard_map/psum | solution.py:102
  256.9 3.9 collective-permute-start.4
  265.2 2.3 gather_fusion.1
  267.5 4.6 fusion.117
  275.6 69.8 %psum.66 = f32[]{:T(128)} all-reduce(f32[]{:T(128)} %get-tuple-element.18), channel_id=1, replica_groups=mesh['seg'=4,'sec'=32,'rep'=2] {'sec'}, use_global_device_ids=true, to_apply=%region_9.0 | all-reduce | flops 1 | bytes 8 | tf_op jit(solution)/shard_map/psum | solution.py:102
  346.9 72.7 %psum.67 = f32[]{:T(128)} all-reduce(f32[]{:T(128)} %get-tuple-element.12), channel_id=1, replica_groups=mesh['seg'=4,'sec'=32,'rep'=2] {'sec'}, use_global_device_ids=true, to_apply=%region_11.0 | all-reduce | flops 1 | bytes 8 | tf_op jit(solution)/shard_map/psum | solution.py:102
  422.2 3.9 collective-permute-start.6
  430.6 2.3 gather_fusion.2
  432.9 4.6 fusion.126
  440.9 70.0 %psum.68 = f32[]{:T(128)} all-reduce(f32[]{:T(128)} %get-tuple-element.20), channel_id=1, replica_groups=mesh['seg'=4,'sec'=32,'rep'=2] {'sec'}, use_global_device_ids=true, to_apply=%region_14.0 | all-reduce | flops 1 | bytes 8 | tf_op jit(solution)/shard_map/psum | solution.py:102
  512.3 72.7 %psum.69 = f32[]{:T(128)} all-reduce(f32[]{:T(128)} %get-tuple-element.10), channel_id=1, replica_groups=mesh['seg'=4,'sec'=32,'rep'=2] {'sec'}, use_global_device_ids=true, to_apply=%region_16.0 | all-reduce | flops 1 | bytes 8 | tf_op jit(solution)/shard_map/psum | solution.py:102
  587.7 3.9 collective-permute-start.8
  596.0 2.3 gather_fusion.3
  598.4 4.6 fusion.135
  606.4 69.8 %psum.70 = f32[]{:T(128)} all-reduce(f32[]{:T(128)} %get-tuple-element.22), channel_id=1, replica_groups=mesh['seg'=4,'sec'=32,'rep'=2] {'sec'}, use_global_device_ids=true, to_apply=%region_19.0 | all-reduce | flops 1 | bytes 8 | tf_op jit(solution)/shard_map/psum | solution.py:102
  677.6 72.7 %psum.71 = f32[]{:T(128)} all-reduce(f32[]{:T(128)} %get-tuple-element.8), channel_id=1, replica_groups=mesh['seg'=4,'sec'=32,'rep'=2] {'sec'}, use_global_device_ids=true, to_apply=%region_21.0 | all-reduce | flops 1 | bytes 8 | tf_op jit(solution)/shard_map/psum | solution.py:102
  (73 shorter events, 44.7 us)
Async XLA Ops:
  0.6 93.0 %copy-start = (bf16[1,2,256,256]{3,2,1,0:T(8,128)(2,1)S(1)}, bf16[1,2,256,256]{3,2,1,0:T(8,128)(2,1)}, u32[]{:S(2)}) copy-start(bf16[1,2,256,256]{3,2,1,0:T(8,128)(2,1)} %param.11) | copy-start | bytes 786436
  0.6 6.2 copy-start.1
  4.1 4.4 copy-start.2
  4.1 4.6 copy-start.4
  4.1 4.6 copy-start.5
  4.1 97.9 %collective-permute-start.3 = (bf16[1,9,2,256,256]{4,3,1,2,0:T(8,128)(2,1)}, bf16[1,9,2,256,256]{4,3,1,2,0:T(8,128)(2,1)}, u32[]{:S(2)}, u32[]{:S(2)}) collective-permute-start(bf16[1,9,2,256,256]{4,3,1,2,0:T(8,128)(2,1)} %copy.35), channel_id=1, source_target_pairs={{0,192},{64,0},{128,64},{192,128},{1,193},{65,1},{129,65},{193,129... | collective-permute-start | bytes 7077896 | tf_op jit(solution)/shard_map/ppermute | solution.py:33
  8.5 84.8 %copy-start.6 = (s32[18]{0:T(128)S(1)}, s32[18]{0:T(128)}, u32[]{:S(2)}) copy-start(s32[18]{0:T(128)} %param.15) | copy-start | bytes 220
  8.5 85.1 %copy-start.3 = (s32[1,9,2]{1,2,0:T(2,128)S(1)}, s32[1,9,2]{1,2,0:T(2,128)}, u32[]{:S(2)}) copy-start(s32[1,9,2]{1,2,0:T(2,128)} %param.14) | copy-start | bytes 220
  8.5 93.5 %collective-permute-start.2 = (bf16[1,9,2,256,256]{4,3,1,2,0:T(8,128)(2,1)}, bf16[1,9,2,256,256]{4,3,1,2,0:T(8,128)(2,1)}, u32[]{:S(2)}, u32[]{:S(2)}) collective-permute-start(bf16[1,9,2,256,256]{4,3,1,2,0:T(8,128)(2,1)} %copy.33), channel_id=1, source_target_pairs={{0,64},{64,128},{128,192},{192,0},{1,65},{65,129},{129,193},{193,1... | collective-permute-start | bytes 7077896 | tf_op jit(solution)/shard_map/ppermute | solution.py:33
  85.0 10.3 %collective-permute-start.1 = (bf16[2,256,256]{1,2,0:T(8,128)(2,1)S(1)}, bf16[2,256,256]{1,2,0:T(8,128)(2,1)S(1)}, u32[]{:S(2)}, u32[]{:S(2)}) collective-permute-start(bf16[2,256,256]{1,2,0:T(8,128)(2,1)S(1)} %fusion.159), channel_id=1, source_target_pairs={{2,0},{4,2},{6,4},{8,6},{10,8},{12,10},{14,12},{16,14},{18,16},{20... | collective-permute-start | bytes 786440 | tf_op jit(solution)/shard_map/ppermute | solution.py:26
  91.4 8.3 %collective-permute-start = (bf16[2,256,256]{1,2,0:T(8,128)(2,1)S(1)}, bf16[2,256,256]{1,2,0:T(8,128)(2,1)S(1)}, u32[]{:S(2)}, u32[]{:S(2)}) collective-permute-start(bf16[2,256,256]{1,2,0:T(8,128)(2,1)S(1)} %fusion.159), channel_id=1, source_target_pairs={{0,2},{2,4},{4,6},{6,8},{8,10},{10,12},{12,14},{14,16},{16,18},{18... | collective-permute-start | bytes 786440 | tf_op jit(solution)/shard_map/ppermute | solution.py:25
  254.9 8.3 %collective-permute-start.5 = (bf16[2,256,256]{1,2,0:T(8,128)(2,1)S(1)}, bf16[2,256,256]{1,2,0:T(8,128)(2,1)S(1)}, u32[]{:S(2)}, u32[]{:S(2)}) collective-permute-start(bf16[2,256,256]{1,2,0:T(8,128)(2,1)S(1)} %get-tuple-element.14), channel_id=1, source_target_pairs={{2,0},{4,2},{6,4},{8,6},{10,8},{12,10},{14,12},{16,14},{18,16},{20... | collective-permute-start | bytes 786440 | tf_op jit(solution)/shard_map/ppermute | solution.py:26
  256.9 8.3 %collective-permute-start.4 = (bf16[2,256,256]{1,2,0:T(8,128)(2,1)S(1)}, bf16[2,256,256]{1,2,0:T(8,128)(2,1)S(1)}, u32[]{:S(2)}, u32[]{:S(2)}) collective-permute-start(bf16[2,256,256]{1,2,0:T(8,128)(2,1)S(1)} %get-tuple-element.14), channel_id=1, source_target_pairs={{0,2},{2,4},{4,6},{6,8},{8,10},{10,12},{12,14},{14,16},{16,18},{18... | collective-permute-start | bytes 786440 | tf_op jit(solution)/shard_map/ppermute | solution.py:25
  420.3 8.3 %collective-permute-start.7 = (bf16[2,256,256]{1,2,0:T(8,128)(2,1)S(1)}, bf16[2,256,256]{1,2,0:T(8,128)(2,1)S(1)}, u32[]{:S(2)}, u32[]{:S(2)}) collective-permute-start(bf16[2,256,256]{1,2,0:T(8,128)(2,1)S(1)} %fusion.158), channel_id=1, source_target_pairs={{2,0},{4,2},{6,4},{8,6},{10,8},{12,10},{14,12},{16,14},{18,16},{20... | collective-permute-start | bytes 786440 | tf_op jit(solution)/shard_map/ppermute | solution.py:26
  422.2 8.3 %collective-permute-start.6 = (bf16[2,256,256]{1,2,0:T(8,128)(2,1)S(1)}, bf16[2,256,256]{1,2,0:T(8,128)(2,1)S(1)}, u32[]{:S(2)}, u32[]{:S(2)}) collective-permute-start(bf16[2,256,256]{1,2,0:T(8,128)(2,1)S(1)} %fusion.158), channel_id=1, source_target_pairs={{0,2},{2,4},{4,6},{6,8},{8,10},{10,12},{12,14},{14,16},{16,18},{18... | collective-permute-start | bytes 786440 | tf_op jit(solution)/shard_map/ppermute | solution.py:25
  585.7 8.3 %collective-permute-start.9 = (bf16[2,256,256]{1,2,0:T(8,128)(2,1)S(1)}, bf16[2,256,256]{1,2,0:T(8,128)(2,1)S(1)}, u32[]{:S(2)}, u32[]{:S(2)}) collective-permute-start(bf16[2,256,256]{1,2,0:T(8,128)(2,1)S(1)} %fusion.157), channel_id=1, source_target_pairs={{2,0},{4,2},{6,4},{8,6},{10,8},{12,10},{14,12},{16,14},{18,16},{20... | collective-permute-start | bytes 786440 | tf_op jit(solution)/shard_map/ppermute | solution.py:26
  587.7 8.3 %collective-permute-start.8 = (bf16[2,256,256]{1,2,0:T(8,128)(2,1)S(1)}, bf16[2,256,256]{1,2,0:T(8,128)(2,1)S(1)}, u32[]{:S(2)}, u32[]{:S(2)}) collective-permute-start(bf16[2,256,256]{1,2,0:T(8,128)(2,1)S(1)} %fusion.157), channel_id=1, source_target_pairs={{0,2},{2,4},{4,6},{6,8},{8,10},{10,12},{12,14},{14,16},{16,18},{18... | collective-permute-start | bytes 786440 | tf_op jit(solution)/shard_map/ppermute | solution.py:25
